TPU v7x, 256 devices: a whole 4x4x8 slice. The times are simulated.
256 devices in a mesh: date: 16 (over z, core), path: 16 (over x, y).
Axes of the slice: x: 4, y: 4, z: 8, core: 2. Of those that a mesh axis runs over, the one named last changes fastest.
Arguments:
- features: bfloat16 [32, 2048, 2048], P('date', 'path'), may hold values from -6 to 6
- payoff: float32 [32, 2048, 256], P('date', 'path'), may hold values from -8 to 64
- coefficients: bfloat16 [2048, 256], replicated, may hold values from -0.02734375 to 0.02734375
- exercise: int32 [32, 256], P('date'), may hold values from 0 to 1, as said below
Outputs:
- gradient: float32 [2048, 256], P(('date', 'path'))
- bound: float32 [256], replicated
- spread: float32 [256], replicated
Inputs may be any that keep to these rules, and one draw needn't show every extreme that they name: `exercise`: every contract may be exercised at the first and at the last date.
All inputs are finite; a program needn't handle non-finite values.
Results may differ from a plain program's by a relative error of at most 0.0017.
Values sent between devices are 32-bit elements; how exact they have to be, the bound alone decides.
A program may use at most 64 MiB of HBM per device.

v0:
```python
import jax
import jax.numpy as jnp
from jax import lax
from jax.sharding import Mesh
from jax.sharding import PartitionSpec as P

PATH = ("path_0", "path_1")
DATE = ("date_0", "date_1")
DATE_PATH = ("date_0", "date_1", "path_0", "path_1")


TEMP = 0.25
NEG = -1e30


def neutral_like(value, identity):
    return jnp.broadcast_to(jnp.asarray(identity, value.dtype), value.shape)


def carried_in(value, axes, combine, identity, reverse):
    before = start = neutral_like(value, identity)
    total = value
    for axis in reversed(axes):
        peers, here = (lax.axis_size(axis), lax.axis_index(axis))
        pieces = lax.all_gather(total, axis)
        inside, total = (start, start)
        for k in reversed(range(peers)) if reverse else range(peers):
            passed = k > here if reverse else k < here
            total = combine(total, pieces[k])
            inside = jnp.where(passed, total, inside)
        before = combine(inside, before)
    return before


def gathered_total(value, axis):
    return lax.all_gather(value, axis).max(0)


def over_pieces(value, axis):
    return lax.all_gather(value, axis).sum(0)


def cut_along(value, dim, peers):
    lengths = value.shape
    blocks = value.reshape(*lengths[:dim], peers, lengths[dim] // peers, *lengths[dim + 1 :])
    return jnp.moveaxis(blocks, dim, 0)


def sum_at_owner(value, axis, dim):
    blocks = cut_along(value, dim, lax.axis_size(axis))
    arrived = lax.all_to_all(blocks, axis, split_axis=0, concat_axis=0, tiled=True)
    return arrived.sum(axis=0)


def one_axis_at_a_time(value, axes):
    for axis in axes:
        value = lax.psum(value, axis)
    return value


def shards(features, payoff, coefficients, exercise):
    dates_dev, paths_dev, width = features.shape
    contracts = coefficients.shape[1]
    paths_total = paths_dev * lax.axis_size(PATH)
    flat = features.reshape(-1, width)
    increments = jnp.dot(flat, coefficients, preferred_element_type=jnp.float32).reshape(
        dates_dev, paths_dev, contracts
    )
    local_sums = jnp.cumsum(increments, axis=0)
    block_total = local_sums[-1]
    earlier = carried_in(block_total, DATE, lambda a, b: a + b, jnp.zeros_like(block_total), False)
    martingale = local_sums + earlier[None]
    allowed = exercise[:, None, :] > 0
    score = jnp.where(allowed, (payoff - martingale) / TEMP, NEG)
    local_peak = jnp.max(score, axis=0)
    peak = gathered_total(local_peak, DATE)
    shifted = jnp.exp(score - peak[None])
    total = over_pieces(jnp.sum(shifted, axis=0), DATE)
    smoothed = TEMP * (peak + jnp.log(total))
    weight = shifted / total[None]
    local_tail = jnp.flip(jnp.cumsum(jnp.flip(weight, 0), axis=0), 0)
    later = carried_in(local_tail[0], DATE, lambda a, b: a + b, jnp.zeros_like(local_tail[0]), True)
    tail = (local_tail + later[None]).astype(jnp.bfloat16).reshape(-1, contracts)
    columns = features.reshape(-1, width // lax.axis_size(DATE) * lax.axis_size(DATE))
    product = jnp.dot(columns.T, tail, preferred_element_type=jnp.float32)
    partial_rows = sum_at_owner(-product / paths_total, DATE, 0)
    gradient = sum_at_owner(partial_rows, PATH, 0)
    first_sum, second_sum = (
        one_axis_at_a_time(jnp.sum(smoothed, axis=0), PATH),
        one_axis_at_a_time(jnp.sum(smoothed * smoothed, axis=0), PATH),
    )
    bound = first_sum / paths_total
    spread = second_sum / paths_total - bound * bound
    return (gradient, bound, spread)


def solution(mesh):
    torus = Mesh(mesh.devices.reshape(8, 2, 4, 4), ("date_0", "date_1", "path_0", "path_1"))
    in_specs = (P(DATE, PATH, None), P(DATE, PATH, None), P(), P(DATE, None))
    out_specs = (P(DATE_PATH, None), P(), P())
    return jax.shard_map(
        shards, mesh=torus, in_specs=in_specs, out_specs=out_specs, check_vma=False
    )
```

profile of v0, /device:TPU:1, one launch (start us, length us, event | category | flops | bytes accessed | tf_op | source)
XLA Modules:
  0.0 255.9 jit_solution(18293468339244961872)
XLA Ops:
  7.2 0.0 copy-start
  7.2 0.0 copy-start.2
  7.2 0.0 all-gather.7.cloned.1.call-start
  7.2 1.2 copy-done
  8.4 1.7 fusion.3
  10.1 0.0 copy-start.1
  10.1 0.1 fusion.15
  10.2 4.8 %all_gather.26 = f32[2,128,256]{2,1,0:T(8,128)S(1)} all-gather(f32[1,128,256]{2,1,0:T(8,128)S(1)} %slice.89), channel_id=1, replica_groups=mesh['date_0'=8,'date_1'=2,'path_0'=4,'path_1'=4] {'date_1'}, dimensions={0}, use_global_device_ids=true | all-gather | bytes 393216 | tf_op jit(solution)/shard_map/all_gather | solution.py:25
  15.1 0.7 slice_add_fusion.15
  15.7 0.0 all-gather.7.cloned.1.call-update
  15.7 0.0 all-gather.11.cloned.1.call-start
  15.8 0.0 copy-done.2
  15.8 34.4 %all-gather.7.cloned.1.call-done = f32[8,128,256]{2,1,0:T(8,128)} async-done(((f32[1,128,256]{2,1,0:T(8,128)}), f32[8,128,256]{2,1,0:T(8,128)}) %all-gather.7.cloned.1.call-update) | async-done | bytes 1048592 | tf_op jit(solution)/shard_map/all_gather | solution.py:25
  50.2 1.4 fusion.12
  51.6 0.0 copy-done.1
  51.6 0.7 fusion.14
  52.3 0.0 all-gather.11.cloned.1.call-update
  52.4 0.0 all-gather.13.cloned.1.call-start
  52.4 43.4 %all-gather.11.cloned.1.call-done = f32[2048,256]{1,0:T(8,128)} async-done(((f32[128,256]{1,0:T(8,128)}), f32[2048,256]{1,0:T(8,128)}) %all-gather.11.cloned.1.call-update) | async-done | bytes 2097168 | tf_op jit(solution)/shard_map/all_gather | solution.py:36
  95.8 1.7 reduce_max.19
  97.5 0.7 fusion.6
  98.2 0.0 all-gather.13.cloned.1.call-update
  98.2 0.0 all-gather.9.cloned.1.call-start
  98.3 37.9 %all-gather.13.cloned.1.call-done = f32[2048,256]{1,0:T(8,128)} async-done(((f32[128,256]{1,0:T(8,128)}), f32[2048,256]{1,0:T(8,128)}) %all-gather.13.cloned.1.call-update) | async-done | bytes 2097168 | tf_op jit(solution)/shard_map/all_gather | solution.py:40
  136.2 1.7 reduce_sum.55
  137.9 0.1 fusion.5
  138.0 0.1 fusion.16
  138.2 2.0 all_gather.32
  140.2 0.7 slice_add_fusion.7
  140.8 0.0 all-gather.9.cloned.1.call-update
  140.9 31.5 %all-gather.9.cloned.1.call-done = f32[8,128,256]{2,1,0:T(8,128)} async-done(((f32[1,128,256]{2,1,0:T(8,128)}), f32[8,128,256]{2,1,0:T(8,128)}) %all-gather.9.cloned.1.call-update) | async-done | bytes 1048592 | tf_op jit(solution)/shard_map/all_gather | solution.py:25
  172.4 1.4 fusion.9
  173.8 0.5 fusion.2
  174.2 1.6 copy.23
  175.8 9.8 %all-to-all-start = ((f32[16,128,256]{1,2,0:T(8,128)}), f32[16,128,256]{1,2,0:T(8,128)S(1)}, u32[]{:S(2)}, u32[]{:S(2)}) async-start(f32[16,128,256]{1,2,0:T(8,128)} %bitcast.29), calls=%async_computation | async-start | bytes 4194304 | tf_op jit(solution)/shard_map/all_to_all | solution.py:51
  185.6 0.1 multiply_reduce_fusion
  185.7 8.7 %all-reduce.1 = (f32[256]{0:T(256)S(1)}, f32[256]{0:T(256)S(1)}) all-reduce(f32[256]{0:T(256)S(1)} %get-tuple-element.4, f32[256]{0:T(256)S(1)} %get-tuple-element.3), channel_id=1, replica_groups=mesh['date_0'=8,'date_1'=2,'path_0'=4,'path_1'=4] {'path_0'}, use_global_device_ids=true, to_apply=%region_9.10 | all-reduce | flops 512 | bytes 4096 | tf_op jit(solution)/shard_map/psum | solution.py:57
  194.4 9.0 %all-reduce = (f32[256]{0:T(256)S(1)}, f32[256]{0:T(256)S(1)}) all-reduce(f32[256]{0:T(256)S(1)} %get-tuple-element.7, f32[256]{0:T(256)S(1)} %get-tuple-element.8), channel_id=1, replica_groups=mesh['date_0'=8,'date_1'=2,'path_0'=4,'path_1'=4] {'path_1'}, use_global_device_ids=true, to_apply=%region_10.11 | all-reduce | flops 512 | bytes 4096 | tf_op jit(solution)/shard_map/psum | solution.py:57
  203.4 31.3 %all-to-all-done = f32[16,128,256]{1,2,0:T(8,128)S(1)} async-done(((f32[16,128,256]{1,2,0:T(8,128)}), f32[16,128,256]{1,2,0:T(8,128)S(1)}, u32[]{:S(2)}, u32[]{:S(2)}) %all-to-all-start) | async-done | bytes 2097184 | tf_op jit(solution)/shard_map/all_to_all | solution.py:51
  234.7 0.1 reduce_sum.56
  234.8 0.7 copy.18
  235.5 6.5 %all-to-all-start.1 = ((f32[16,8,256]{2,1,0:T(8,128)}), f32[16,8,256]{2,1,0:T(8,128)S(1)}, u32[]{:S(2)}, u32[]{:S(2)}) async-start(f32[16,8,256]{2,1,0:T(8,128)} %bitcast.7), calls=%async_computation.1 | async-start | bytes 262144 | tf_op jit(solution)/shard_map/all_to_all | solution.py:51
  242.1 0.6 multiply_subtract_fusion
  242.6 6.1 %all-to-all-done.1 = f32[16,8,256]{2,1,0:T(8,128)S(1)} async-done(((f32[16,8,256]{2,1,0:T(8,128)}), f32[16,8,256]{2,1,0:T(8,128)S(1)}, u32[]{:S(2)}, u32[]{:S(2)}) %all-to-all-start.1) | async-done | bytes 131104 | tf_op jit(solution)/shard_map/all_to_all | solution.py:51
  248.8 0.6 reduce_sum.57
  (5 shorter events, 0.1 us)
Async XLA Ops:
  7.2 1.2 copy-start
  7.2 8.6 %copy-start.2 = (s32[2,256]{1,0:T(2,128)S(1)}, s32[2,256]{1,0:T(2,128)}, u32[]{:S(2)}) copy-start(s32[2,256]{1,0:T(2,128)} %param.7) | copy-start | bytes 6148
  7.2 43.1 %all-gather.7.cloned.1.call-start = ((), (), s32[]{:S(2)}) async-start(), calls=%async_computation.2 | async-start | bytes 1179648 | tf_op jit(solution)/shard_map/all_gather | solution.py:25
  10.1 41.6 %copy-start.1 = (f32[2,128,256]{2,1,0:T(8,128)S(1)}, f32[2,128,256]{2,1,0:T(8,128)}, u32[]{:S(2)}) copy-start(f32[2,128,256]{2,1,0:T(8,128)} %param.5) | copy-start | bytes 786436
  15.7 80.0 %all-gather.11.cloned.1.call-start = ((), (), s32[]{:S(2)}) async-start(), calls=%async_computation.4 | async-start | bytes 2228224 | tf_op jit(solution)/shard_map/all_gather | solution.py:36
  52.4 83.8 %all-gather.13.cloned.1.call-start = ((), (), s32[]{:S(2)}) async-start(), calls=%async_computation.5 | async-start | bytes 2228224 | tf_op jit(solution)/shard_map/all_gather | solution.py:40
  98.2 74.2 %all-gather.9.cloned.1.call-start = ((), (), s32[]{:S(2)}) async-start(), calls=%async_computation.3 | async-start | bytes 1179648 | tf_op jit(solution)/shard_map/all_gather | solution.py:25
  175.8 58.9 %all-to-all-start = ((f32[16,128,256]{1,2,0:T(8,128)}), f32[16,128,256]{1,2,0:T(8,128)S(1)}, u32[]{:S(2)}, u32[]{:S(2)}) async-start(f32[16,128,256]{1,2,0:T(8,128)} %bitcast.29), calls=%async_computation | async-start | bytes 4194304 | tf_op jit(solution)/shard_map/all_to_all | solution.py:51
  235.5 13.2 %all-to-all-start.1 = ((f32[16,8,256]{2,1,0:T(8,128)}), f32[16,8,256]{2,1,0:T(8,128)S(1)}, u32[]{:S(2)}, u32[]{:S(2)}) async-start(f32[16,8,256]{2,1,0:T(8,128)} %bitcast.7), calls=%async_computation.1 | async-start | bytes 262144 | tf_op jit(solution)/shard_map/all_to_all | solution.py:51
Sparse Core Ops, SparseCore 0:
  15.9 34.3 all-gather.6
  52.5 43.2 all-gather.10
  98.3 37.8 all-gather.12
  141.0 31.3 all-gather.8
where the time goes:
time: 256 us
  waiting for transfers between devices  185 us (72%)
  blocking collectives  24.5 us (10%)
  starting transfers between devices  16.5 us (6%)
  between operations  13.9 us (5%)
  other arithmetic  10.6 us (4%)
  local copies, waits for them, and re-layouts  3.52 us (1%)
    all_gather x2, waiting for transfers between devices, carried_in(): pieces = lax.all_gather(total, axis)  65.9 us
    all_gather x1, waiting for transfers between devices, gathered_total(): return lax.all_gather(value, axis).max(0)  43.4 us
    all_gather x1, waiting for transfers between devices, over_pieces(): return lax.all_gather(value, axis).sum(0)  37.9 us
    all_to_all x2, waiting for transfers between devices, sum_at_owner(): lax.all_to_all(blocks, axis, split_axis=0, concat_axis=0, tiled=True)  37.4 us
    psum x2, blocking collectives, one_axis_at_a_time(): value = lax.psum(value, axis)  17.7 us
    all_to_all x2, starting transfers between devices, sum_at_owner(): lax.all_to_all(blocks, axis, split_axis=0, concat_axis=0, tiled=True)  16.4 us
    all_gather x2, blocking collectives, carried_in(): pieces = lax.all_gather(total, axis)  6.82 us
  transfers between devices with their start and end apart: 6, of which 6 were waited for; matrix products, arithmetic and copies ran while one was open for 0% of the time, Pallas kernels for 0%

commit v1 on v0

v1 whole, which is shorter than its diff:
```python
import functools

import jax
import jax.numpy as jnp
from jax import lax
from jax.experimental import pallas as pl
from jax.experimental.pallas import tpu as pltpu
from jax.sharding import Mesh
from jax.sharding import PartitionSpec as P

DATE = ("z", "core")
PATH = ("x", "y")
AXES = ("z", "core", "x", "y")
NZ, NC, NX, NY = 8, 2, 4, 4
ND = NZ * NC
TEMP = 0.25
MASKED = -1e30 * TEMP
PATHS = 2048
K = 2048
C = 256
R = 8
F32 = jnp.float32
BF16 = jnp.bfloat16
MESH = pl.DeviceIdType.MESH


def body(
    feat,
    pay,
    coef,
    exer,
    grad,
    bound,
    spread,
    fbuf,
    cbuf,
    pbuf,
    ebuf,
    mpay,
    inc,
    pay_all,
    inc_all,
    tail_all,
    tail_in,
    ft,
    other_part,
    other_got,
    part,
    got1,
    sum1,
    got2,
    sum2,
    got3,
    stat,
    stat_c,
    stat_1,
    stat_2,
    stat_3,
    load_sem,
    pay_s,
    pay_r,
    inc_s,
    inc_r,
    tail_s,
    tail_r,
    half_s,
    half_r,
    one_s,
    one_r,
    two_s,
    two_r,
    three_s,
    three_r,
    stat_s,
    stat_r,
):
    z, core, x, y = (lax.axis_index(a) for a in AXES)
    d = z * NC + core
    other = 1 - core

    loads = [
        pltpu.make_async_copy(pay, pbuf, load_sem.at[0]),
        pltpu.make_async_copy(exer, ebuf, load_sem.at[1]),
        pltpu.make_async_copy(coef, cbuf, load_sem.at[2]),
        pltpu.make_async_copy(feat, fbuf, load_sem.at[3]),
    ]
    for copy in loads:
        copy.start()

    def date_peer(i):
        e = lax.rem(d + i, ND)
        return e, (e // NC, lax.rem(e, NC), x, y)

    a = (1 - core) * x + core * y
    b = (1 - core) * y + core * x

    def first_peer(i):
        e = lax.rem(a + i, NX)
        return e, (z, core, (1 - core) * e + core * x, (1 - core) * y + core * e)

    def second_peer(i):
        e = lax.rem(b + i, NX)
        return e, (z, core, (1 - core) * x + core * e, (1 - core) * e + core * y)

    def third_peer(i):
        e = lax.rem(z + i, NZ)
        return e, (e, core, x, y)

    def x_peer(i):
        e = lax.rem(x + i, NX)
        return e, (z, core, e, y)

    def y_peer(i):
        e = lax.rem(y + i, NY)
        return e, (z, core, x, e)

    barrier = pltpu.get_barrier_semaphore()

    @pl.loop(1, ND)
    def _(i):
        pl.semaphore_signal(barrier, inc=1, device_id=date_peer(i)[1], device_id_type=MESH)

    @pl.loop(1, NX)
    def _(i):
        pl.semaphore_signal(barrier, inc=1, device_id=first_peer(i)[1], device_id_type=MESH)
        pl.semaphore_signal(barrier, inc=1, device_id=second_peer(i)[1], device_id_type=MESH)

    loads[0].wait()
    loads[1].wait()
    for t in range(2):
        mpay[t] = jnp.where(ebuf[t : t + 1] > 0, pbuf[t], MASKED)

    pl.semaphore_wait(barrier, ND - 1 + 2 * (NX - 1))

    def mine(ref, e):
        return ref.at[:, pl.ds(pl.multiple_of(e * R, R), R), :]

    def date_copy(src, dst, ssem, rsem, i):
        e, dev = date_peer(i)
        return pltpu.make_async_remote_copy(
            src(e), dst, ssem.at[i - 1], rsem.at[i - 1], device_id=dev, device_id_type=MESH
        )

    def date_wait(src, dst, ssem, rsem, i):
        dev = date_peer(i)[1]
        return pltpu.make_async_remote_copy(
            src(date_peer(i)[0]), dst(lax.rem(d + ND - i, ND)), ssem.at[i - 1], rsem.at[i - 1], device_id=dev, device_id_type=MESH
        )

    @pl.loop(1, ND)
    def _(i):
        date_copy(lambda e: mine(mpay, e), pay_all.at[d], pay_s, pay_r, i).start()

    loads[2].wait()
    loads[3].wait()
    inc[...] = jnp.dot(fbuf[...].reshape(2 * 128, K), cbuf[...], preferred_element_type=F32).reshape(2, 128, C)

    @pl.loop(1, ND)
    def _(i):
        date_copy(lambda e: mine(inc, e), inc_all.at[d], inc_s, inc_r, i).start()

    here = pl.ds(pl.multiple_of(d * R, R), R)
    pay_all[d] = mpay[:, here, :]
    inc_all[d] = inc[:, here, :]

    for k in range(8):
        strip = fbuf[:, :, k * 256 : (k + 1) * 256].reshape(256, 256)
        ft[k * 256 : (k + 1) * 256, :] = strip.T

    @pl.loop(1, ND)
    def _(i):
        date_wait(lambda e: mine(mpay, e), lambda e: pay_all.at[e], pay_s, pay_r, i).wait_recv()
        date_wait(lambda e: mine(inc, e), lambda e: inc_all.at[e], inc_s, inc_r, i).wait_recv()

    total = jnp.zeros((R, C), F32)
    scores = []
    peak = None
    for t in range(2 * ND):
        total = total + inc_all[t // 2, t % 2]
        score = (pay_all[t // 2, t % 2] - total) / TEMP
        peak = score if peak is None else jnp.maximum(peak, score)
        scores.append(score)
    weights = [jnp.exp(s - peak) for s in scores]
    total = functools.reduce(lambda p, q: p + q, weights)
    scale = 1.0 / total
    run = jnp.zeros((R, C), F32)
    for t in reversed(range(2 * ND)):
        run = run + weights[t] * scale
        tail_all[t // 2, t % 2] = run
    smoothed = TEMP * (peak + jnp.log(total))
    stat[0] = jnp.zeros((R, C), F32)
    stat[0, 0:1] = jnp.sum(smoothed, axis=0, keepdims=True)
    stat[0, 1:2] = jnp.sum(smoothed * smoothed, axis=0, keepdims=True)

    @pl.loop(1, ND)
    def _(i):
        date_copy(lambda e: tail_all.at[e], mine(tail_in, d), tail_s, tail_r, i).start()

    tail_in[:, here, :] = tail_all[d]
    partner = (z, other, x, y)
    pair = pltpu.make_async_remote_copy(
        stat.at[0], stat_c, stat_s.at[0], stat_r.at[0], device_id=partner, device_id_type=MESH
    )
    pair.start()

    @pl.loop(1, ND)
    def _(i):
        date_wait(lambda e: tail_all.at[e], lambda e: mine(tail_in, e), tail_s, tail_r, i).wait_recv()

    tail = tail_in[...].reshape(256, C).astype(BF16)

    def half_copy(k):
        return pltpu.make_async_remote_copy(
            other_part.at[k], other_got.at[k], half_s.at[k], half_r.at[k], device_id=partner, device_id_type=MESH
        )

    def product(k, which, out):
        rows = ft[pl.ds(pl.multiple_of(k * 256 + which * 128, 128), 128), :]
        block = jnp.dot(rows, tail, preferred_element_type=F32)
        for p in range(NX):
            for q in range(NY):
                n = (p * NY + q) * R
                out[k, (1 - which) * p + which * q, (1 - which) * q + which * p] = block[n : n + R]

    @pl.loop(0, NZ)
    def _(k):
        product(k, other, other_part)
        half_copy(k).start()

    @pl.loop(0, NZ)
    def _(k):
        product(k, core, part)

    pair.wait_recv()
    stat[1] = stat[0] + stat_c[...]

    @pl.loop(0, NZ)
    def _(k):
        half_copy(k).wait_recv()
        part[k] = part[k] + other_got[k]

    def one_copy(i):
        e, dev = first_peer(i)
        return pltpu.make_async_remote_copy(
            part.at[:, e], got1.at[i - 1], one_s.at[i - 1], one_r.at[i - 1], device_id=dev, device_id_type=MESH
        )

    def two_copy(i):
        e, dev = second_peer(i)
        return pltpu.make_async_remote_copy(
            sum1.at[:, e], got2.at[i - 1], two_s.at[i - 1], two_r.at[i - 1], device_id=dev, device_id_type=MESH
        )

    def three_copy(i):
        e, dev = third_peer(i)
        return pltpu.make_async_remote_copy(
            sum2.at[e], got3.at[i - 1], three_s.at[i - 1], three_r.at[i - 1], device_id=dev, device_id_type=MESH
        )

    def stat_copy(level, got, peer, slot, base, i):
        return pltpu.make_async_remote_copy(
            stat.at[level], got.at[slot], stat_s.at[base + i], stat_r.at[base + i], device_id=peer(i)[1], device_id_type=MESH
        )

    def stat_x(i, arriving=False):
        return stat_copy(1, stat_1, x_peer, lax.rem(x + NX - i, NX) if arriving else x, 0, i)

    def stat_y(i, arriving=False):
        return stat_copy(2, stat_2, y_peer, lax.rem(y + NY - i, NY) if arriving else y, 3, i)

    def stat_z(i, arriving=False):
        return stat_copy(3, stat_3, third_peer, lax.rem(z + NZ - i, NZ) if arriving else z, 6, i)

    def summed(got, n):
        return functools.reduce(lambda p, q: p + q, [got[i] for i in range(n)])

    @pl.loop(1, NX)
    def _(i):
        one_copy(i).start()
        stat_x(i).start()

    @pl.loop(1, NX)
    def _(i):
        one_copy(i).wait_recv()
        stat_x(i, True).wait_recv()

    sum1[...] = ((part[:, a] + got1[0]) + got1[1]) + got1[2]
    stat_1[x] = stat[1]
    stat[2] = summed(stat_1, NX)

    @pl.loop(1, NX)
    def _(i):
        two_copy(i).start()
        stat_y(i).start()

    @pl.loop(1, NX)
    def _(i):
        two_copy(i).wait_recv()
        stat_y(i, True).wait_recv()

    sum2[...] = ((sum1[:, b] + got2[0]) + got2[1]) + got2[2]
    stat_2[y] = stat[2]
    stat[3] = summed(stat_2, NY)

    @pl.loop(1, NZ)
    def _(i):
        three_copy(i).start()
        stat_z(i).start()

    @pl.loop(1, NZ)
    def _(i):
        three_copy(i).wait_recv()
        stat_z(i, True).wait_recv()

    total = sum2[z]
    for i in range(NZ - 1):
        total = total + got3[i]
    stat_3[z] = stat[3]
    sums = summed(stat_3, NZ)
    grad[...] = total * (-1.0 / PATHS)
    mean = sums[0:1] * (1.0 / PATHS)
    bound[...] = mean
    spread[...] = sums[1:2] * (1.0 / PATHS) - mean * mean

    @pl.loop(1, ND)
    def _(i):
        date_copy(lambda e: mine(mpay, e), pay_all.at[d], pay_s, pay_r, i).wait_send()
        date_copy(lambda e: mine(inc, e), inc_all.at[d], inc_s, inc_r, i).wait_send()
        date_copy(lambda e: tail_all.at[e], mine(tail_in, d), tail_s, tail_r, i).wait_send()

    pair.wait_send()

    @pl.loop(0, NZ)
    def _(k):
        half_copy(k).wait_send()

    @pl.loop(1, NX)
    def _(i):
        one_copy(i).wait_send()
        two_copy(i).wait_send()
        stat_x(i).wait_send()
        stat_y(i).wait_send()

    @pl.loop(1, NZ)
    def _(i):
        three_copy(i).wait_send()
        stat_z(i).wait_send()


def shards(features, payoff, coefficients, exercise):
    dma = pltpu.SemaphoreType.DMA
    vmem = pltpu.VMEM
    grad, bound, spread = pl.pallas_call(
        body,
        name="dual_bound",
        out_shape=(
            jax.ShapeDtypeStruct((R, C), F32),
            jax.ShapeDtypeStruct((1, C), F32),
            jax.ShapeDtypeStruct((1, C), F32),
        ),
        in_specs=[pl.BlockSpec(memory_space=pl.ANY)] * 4,
        out_specs=[pl.BlockSpec(memory_space=pltpu.VMEM)] * 3,
        scratch_shapes=[
            vmem((2, 128, K), BF16),
            vmem((K, C), BF16),
            vmem((2, 128, C), F32),
            vmem((2, C), jnp.int32),
            vmem((2, 128, C), F32),
            vmem((2, 128, C), F32),
            vmem((ND, 2, R, C), F32),
            vmem((ND, 2, R, C), F32),
            vmem((ND, 2, R, C), F32),
            vmem((2, 128, C), F32),
            vmem((K, 256), BF16),
            vmem((NZ, NX, NY, R, C), F32),
            vmem((NZ, NX, NY, R, C), F32),
            vmem((NZ, NX, NY, R, C), F32),
            vmem((NX - 1, NZ, NY, R, C), F32),
            vmem((NZ, NY, R, C), F32),
            vmem((NY - 1, NZ, R, C), F32),
            vmem((NZ, R, C), F32),
            vmem((NZ - 1, R, C), F32),
            vmem((4, R, C), F32),
            vmem((R, C), F32),
            vmem((NX, R, C), F32),
            vmem((NY, R, C), F32),
            vmem((NZ, R, C), F32),
            dma((4,)),
            dma((ND - 1,)),
            dma((ND - 1,)),
            dma((ND - 1,)),
            dma((ND - 1,)),
            dma((ND - 1,)),
            dma((ND - 1,)),
            dma((NZ,)),
            dma((NZ,)),
            dma((NX - 1,)),
            dma((NX - 1,)),
            dma((NY - 1,)),
            dma((NY - 1,)),
            dma((NZ - 1,)),
            dma((NZ - 1,)),
            dma((14,)),
            dma((14,)),
        ],
        compiler_params=pltpu.CompilerParams(
            collective_id=0, has_side_effects=True, vmem_limit_bytes=40 * 1024 * 1024
        ),
    )(features, payoff, coefficients, exercise)
    return grad, bound.reshape(C), spread.reshape(C)


def solution(mesh):
    torus = Mesh(mesh.devices.reshape(NZ, NC, NX, NY), AXES)
    in_specs = (P(DATE, PATH, None), P(DATE, PATH, None), P(), P(DATE, None))
    out_specs = (P(DATE + PATH, None), P(), P())
    return jax.shard_map(
        shards, mesh=torus, in_specs=in_specs, out_specs=out_specs, check_vma=False
    )
```

time: 256 us -> 63.1 us (0.25)
  the two profiles are of different devices: /device:TPU:1 before, /device:TPU:32 now
where the time goes in v1:
time: 63.1 us; the launch traced here: 62.9 us
  Pallas kernels  56.4 us (89%)
  local copies, waits for them, and re-layouts  5.8 us (9%)
  between operations  0.65 us (1%)
    pallas_call x1, Pallas kernels, shards(): pl.pallas_call(body, name='dual_bound', out_shape=(jax.ShapeDtypeStruct((...  56.4 us
    unnamed x11, local copies, waits for them, and re-layouts  5.8 us

profile of v1, /device:TPU:32, one launch (start us, length us, event | category | flops | bytes accessed | tf_op | source)
XLA Modules:
  0.0 62.9 jit_solution(14380285012006507361)
XLA Ops:
  0.6 0.0 copy-start
  0.6 1.2 %copy-done = bf16[2,128,2048]{2,1,0:T(8,128)(2,1)S(1)} copy-done((bf16[2,128,2048]{2,1,0:T(8,128)(2,1)S(1)}, bf16[2,128,2048]{2,1,0:T(8,128)(2,1)}, u32[]{:S(2)}) %copy-start) | copy-done | bytes 1048600
  1.9 0.0 copy-start.1
  1.9 1.2 %copy-done.1 = bf16[2048,256]{1,0:T(8,128)(2,1)S(1)} copy-done((bf16[2048,256]{1,0:T(8,128)(2,1)S(1)}, bf16[2048,256]{1,0:T(8,128)(2,1)}, u32[]{:S(2)}) %copy-start.1) | copy-done | bytes 1048600
  3.1 0.0 copy-start.2
  3.1 0.9 %copy-done.2 = f32[2,128,256]{2,1,0:T(8,128)S(1)} copy-done((f32[2,128,256]{2,1,0:T(8,128)S(1)}, f32[2,128,256]{2,1,0:T(8,128)}, u32[]{:S(2)}) %copy-start.2) | copy-done | bytes 262168
  4.0 0.0 copy-start.3
  4.0 0.7 %copy-done.3 = s32[2,256]{1,0:T(2,128)S(1)} copy-done((s32[2,256]{1,0:T(2,128)S(1)}, s32[2,256]{1,0:T(2,128)}, u32[]{:S(2)}) %copy-start.3) | copy-done | bytes 2072
  4.7 56.4 %dual_bound.1 = (f32[8,256]{1,0:T(8,128)S(1)}, f32[1,256]{1,0:T(1,128)S(1)}, f32[1,256]{1,0:T(1,128)S(1)}) custom-call(bf16[2,128,2048]{2,1,0:T(8,128)(2,1)S(1)} %copy-done, f32[2,128,256]{2,1,0:T(8,128)S(1)} %copy-done.2, bf16[2048,256]{1,0:T(8,128)(2,1)S(1)} %copy-done.1, s32[2,256]{1,0:T(2,128)S(1)} %copy-done.3), custom_call_target="tpu_custom_call" | custom-call | tf_op jit(solution)/shard_map/dual_bound/pallas_call | solution.py:353
  61.1 0.6 copy.10
  61.7 0.6 copy.11
  62.3 0.6 copy.12
Async XLA Ops:
  0.6 1.2 %copy-start = (bf16[2,128,2048]{2,1,0:T(8,128)(2,1)S(1)}, bf16[2,128,2048]{2,1,0:T(8,128)(2,1)}, u32[]{:S(2)}) copy-start(bf16[2,128,2048]{2,1,0:T(8,128)(2,1)} %feat.1) | copy-start | bytes 3145732
  1.9 1.2 %copy-start.1 = (bf16[2048,256]{1,0:T(8,128)(2,1)S(1)}, bf16[2048,256]{1,0:T(8,128)(2,1)}, u32[]{:S(2)}) copy-start(bf16[2048,256]{1,0:T(8,128)(2,1)} %coef.1) | copy-start | bytes 3145732
  3.1 0.9 %copy-start.2 = (f32[2,128,256]{2,1,0:T(8,128)S(1)}, f32[2,128,256]{2,1,0:T(8,128)}, u32[]{:S(2)}) copy-start(f32[2,128,256]{2,1,0:T(8,128)} %pay.1) | copy-start | bytes 786436
  4.0 0.7 %copy-start.3 = (s32[2,256]{1,0:T(2,128)S(1)}, s32[2,256]{1,0:T(2,128)}, u32[]{:S(2)}) copy-start(s32[2,256]{1,0:T(2,128)} %exer.1) | copy-start | bytes 6148

commit v2 on v0

v2 whole, which is shorter than its diff:
```python
import functools

import jax
import jax.numpy as jnp
from jax import lax
from jax.experimental import pallas as pl
from jax.experimental.pallas import tpu as pltpu
from jax.sharding import Mesh
from jax.sharding import PartitionSpec as P

DATE = ("z", "core")
PATH = ("x", "y")
AXES = ("z", "core", "x", "y")
NZ, NC, NX, NY = 8, 2, 4, 4
TEMP = 0.25
MASKED = -1e30 * TEMP
PATHS = 2048
K = 2048
C = 256
R = 8
H = 2
W = C // H
F32 = jnp.float32
BF16 = jnp.bfloat16
MESH = pl.DeviceIdType.MESH
ORDER = (2, 1, 3, 0)


def scope(name):
    return jax.named_scope(name)


def body(
    feat,
    pay,
    coef,
    exer,
    grad,
    sums_out,
    fbuf,
    cbuf,
    pbuf,
    ebuf,
    mpay,
    pay_got,
    inc,
    inc_got,
    fx_send,
    fx_got,
    fall,
    ft,
    rel,
    bl,
    bl_all,
    fl,
    fl_in,
    other_part,
    other_got,
    part,
    via_l,
    via_r,
    got_l,
    got_r,
    sum1,
    got2,
    sum2,
    got3,
    stat,
    stat_c,
    stat_1,
    stat_2,
    stat_3,
    load_sem,
    pair_s,
    pair_r,
    bl_s,
    bl_r,
    fl_s,
    fl_r,
    half_s,
    half_r,
    one_s,
    one_r,
    two_s,
    two_r,
    three_s,
    three_r,
    stat_s,
    stat_r,
):
    z, core, x, y = (lax.axis_index(a) for a in AXES)
    other = 1 - core

    loads = [
        pltpu.make_async_copy(coef, cbuf, load_sem.at[0]),
        pltpu.make_async_copy(feat, fbuf, load_sem.at[1]),
        pltpu.make_async_copy(exer, ebuf, load_sem.at[2]),
        pltpu.make_async_copy(pay, pbuf, load_sem.at[3]),
    ]
    for copy in loads:
        copy.start()

    a = (1 - core) * x + core * y
    b = (1 - core) * y + core * x
    a_other = (1 - other) * x + other * y

    def along_a(e):
        return (z, core, (1 - core) * e + core * x, (1 - core) * y + core * e)

    def along_b(e):
        return (z, core, (1 - core) * x + core * e, (1 - core) * e + core * y)

    partner = (z, other, x, y)
    right, left = along_a(lax.rem(a + 1, NX)), along_a(lax.rem(a + NX - 1, NX))

    def b_peer(i):
        e = lax.rem(b + i, NX)
        return e, along_b(e)

    def z_peer(i):
        e = lax.rem(z + i, NZ)
        return e, (e, core, x, y)

    def x_peer(i):
        e = lax.rem(x + i, NX)
        return e, (z, core, e, y)

    def y_peer(i):
        e = lax.rem(y + i, NY)
        return e, (z, core, x, e)

    def remote(src, dst, ssem, rsem, device):
        return pltpu.make_async_remote_copy(src, dst, ssem, rsem, device_id=device, device_id_type=MESH)

    def greet(device):
        pl.semaphore_signal(barrier, inc=1, device_id=device, device_id_type=MESH)

    barrier = pltpu.get_barrier_semaphore()
    with scope("a_signal"):
        greet(partner)

        @pl.loop(1, NZ)
        def _(i):
            greet(z_peer(i)[1])

        @pl.loop(1, NX)
        def _(i):
            greet(x_peer(i)[1])
            greet(y_peer(i)[1])

    with scope("b_mm1"):
        loads[0].wait()
        loads[1].wait()
        flat = fbuf[...].reshape(2 * 128, K)
        incs = jnp.dot(flat, cbuf[...], preferred_element_type=F32)
        for h in range(H):
            inc[h] = incs[:, h * W : (h + 1) * W].reshape(2, 128, W)

    with scope("c_mask"):
        loads[2].wait()
        loads[3].wait()
        for t in range(2):
            mpay[t] = jnp.where(ebuf[t : t + 1] > 0, pbuf[t], MASKED)

    with scope("d_barrier"):
        pl.semaphore_wait(barrier, 1 + NZ - 1 + 2 * (NX - 1))

    own_half = pl.ds(pl.multiple_of(core * 64, 64), 64)
    other_half = pl.ds(pl.multiple_of(other * 64, 64), 64)

    pay_copy = remote(mpay.at[:, other_half, :], pay_got, pair_s.at[0], pair_r.at[0], partner)
    inc_copy = [
        remote(inc.at[h, :, other_half, :], inc_got.at[h], pair_s.at[1 + h], pair_r.at[1 + h], partner) for h in range(H)
    ]
    pay_copy.start()
    for copy in inc_copy:
        copy.start()

    with scope("e_convert"):
        for t in range(2):
            fx_send[t] = fbuf[t, other_half, :].astype(F32)
            fall[2 * core + t] = fbuf[t, own_half, :]

    def bl_copy(h, i):
        e, dev = z_peer(i)
        return remote(bl.at[h, e], bl_all.at[h, z], bl_s.at[h, i - 1], bl_r.at[h, i - 1], dev)

    def bl_wait(h, i):
        e, dev = z_peer(i)
        src = lax.rem(z + NZ - i, NZ)
        return remote(bl.at[h, e], bl_all.at[h, src], bl_s.at[h, i - 1], bl_r.at[h, i - 1], dev)

    def fl_copy(h, i):
        e, dev = z_peer(i)
        return remote(fl.at[h, e], fl_in.at[h, z], fl_s.at[h, i - 1], fl_r.at[h, i - 1], dev)

    def fl_wait(h, i):
        e, dev = z_peer(i)
        src = lax.rem(z + NZ - i, NZ)
        return remote(fl.at[h, e], fl_in.at[h, src], fl_s.at[h, i - 1], fl_r.at[h, i - 1], dev)

    pay_copy.wait_recv()
    for h in range(H):
        with scope("f_blocks%d" % h):
            cols = pl.ds(h * W, W)
            inc_copy[h].wait_recv()
            first = core == 0
            run = jnp.zeros((64, W), F32)
            us = []
            for t in range(4):
                mine_inc, got_inc = inc[h, t % 2, own_half, :], inc_got[h, t % 2]
                mine_pay, got_pay = mpay[t % 2, own_half, cols], pay_got[t % 2, :, cols]
                own = first if t < 2 else jnp.logical_not(first)
                run = run + jnp.where(own, mine_inc, got_inc)
                us.append((jnp.where(own, mine_pay, got_pay) - run) / TEMP)
            top = functools.reduce(jnp.maximum, us)
            lse = top + jnp.log(functools.reduce(lambda p, q: p + q, [jnp.exp(u - top) for u in us]))
            for t in range(4):
                rel[h, t] = us[t]
            for s in range(NZ):
                bl[h, s, 0] = run[s * R : (s + 1) * R]
                bl[h, s, 1] = lse[s * R : (s + 1) * R]

            @pl.loop(1, NZ)
            def _(i):
                bl_copy(h, i).start()

            bl_all[h, z] = bl[h, z]

    fx_copy = remote(fx_send, fx_got, pair_s.at[3], pair_r.at[3], partner)
    fx_copy.start()
    with scope("g_features"):
        fx_copy.wait_recv()
        for t in range(2):
            fall[2 * other + t] = fx_got[t].astype(BF16)
        for k in range(8):
            strip = fall[:, :, k * 256 : (k + 1) * 256].reshape(256, 256).T
            for which in range(2):
                ft[which, k * 128 : (k + 1) * 128, :] = strip[which * 128 : (which + 1) * 128]

    stat[0] = jnp.zeros((R, C), F32)
    for h in range(H):
        with scope("h_blwait%d" % h):

            @pl.loop(1, NZ)
            def _(i):
                bl_wait(h, i).wait_recv()

        with scope("i_owner%d" % h):
            cols = slice(h * W, (h + 1) * W)
            before = jnp.zeros((R, W), F32)
            befores, ss = [], []
            for s in range(NZ):
                shift = before / TEMP
                befores.append(shift)
                ss.append(bl_all[h, s, 1] - shift)
                before = before + bl_all[h, s, 0]
            peak = functools.reduce(jnp.maximum, ss)
            lse = peak + jnp.log(functools.reduce(lambda p, q: p + q, [jnp.exp(s - peak) for s in ss]))
            later = jnp.zeros((R, W), F32)
            for s in reversed(range(NZ)):
                fl[h, s, 0] = lse + befores[s]
                fl[h, s, 1] = later
                later = later + jnp.exp(ss[s] - lse)
            smoothed = TEMP * lse
            stat[0, 0:1, cols] = jnp.sum(smoothed, axis=0, keepdims=True)
            stat[0, 1:2, cols] = jnp.sum(smoothed * smoothed, axis=0, keepdims=True)

            @pl.loop(1, NZ)
            def _(i):
                fl_copy(h, i).start()

            fl_in[h, z] = fl[h, z]

    stat_pair = remote(stat.at[0], stat_c, stat_s.at[0], stat_r.at[0], partner)
    stat_pair.start()

    def half_copy(h, j):
        chunk = lax.rem(a_other + ORDER[j], NX)
        return remote(other_part.at[h, chunk], other_got.at[h, chunk], half_s.at[h, j], half_r.at[h, j], partner)

    def half_wait(h, j):
        chunk = lax.rem(a + ORDER[j], NX)
        return remote(other_part.at[h, chunk], other_got.at[h, chunk], half_s.at[h, j], half_r.at[h, j], partner)

    lo, hi = pl.ds(0, NY // 2), pl.ds(NY // 2, NY // 2)
    two_on = lax.rem(a + 2, NX)
    one_on = lax.rem(a + 1, NX)
    one_back = lax.rem(a + 3, NX)

    def one_copies(h):
        return dict(
            via_r=remote(part.at[h, two_on, lo], via_l.at[h], one_s.at[h, 0], one_r.at[h, 0], right),
            via_l=remote(part.at[h, two_on, hi], via_r.at[h], one_s.at[h, 1], one_r.at[h, 1], left),
            direct_r=remote(part.at[h, one_on, hi], got_l.at[h, hi], one_s.at[h, 2], one_r.at[h, 2], right),
            direct_l=remote(part.at[h, one_back, lo], got_r.at[h, lo], one_s.at[h, 3], one_r.at[h, 3], left),
            comb_r=remote(part.at[h, one_on, lo], got_l.at[h, lo], one_s.at[h, 4], one_r.at[h, 4], right),
            comb_l=remote(part.at[h, one_back, hi], got_r.at[h, hi], one_s.at[h, 5], one_r.at[h, 5], left),
        )

    one = [one_copies(h) for h in range(H)]

    def product(h, which, tail, out):
        for n in range(2):
            block = jnp.dot(ft[which, n * 512 : (n + 1) * 512, :], tail, preferred_element_type=F32)
            for k in range(4):
                for p in range(NX):
                    for q in range(NY):
                        row = k * 128 + (p * NY + q) * R
                        out[h, (1 - which) * p + which * q, (1 - which) * q + which * p, n * 4 + k] = block[row : row + R]

    for h in range(H):
        with scope("j_flwait%d" % h):

            @pl.loop(1, NZ)
            def _(i):
                fl_wait(h, i).wait_recv()

        with scope("k_mm2a%d" % h):
            level = fl_in[h, :, 0].reshape(64, W)
            run = fl_in[h, :, 1].reshape(64, W)
            tails = [None] * 4
            for t in reversed(range(4)):
                run = run + jnp.exp(rel[h, t] - level)
                tails[t] = run.astype(BF16)
            tail = jnp.concatenate(tails, axis=0)
            product(h, other, tail, other_part)
            for j in range(NX):
                half_copy(h, j).start()
        with scope("l_mm2b%d" % h):
            product(h, core, tail, part)
        with scope("m_half%d" % h):
            half_wait(h, 0).wait_recv()
            part[h, two_on] = part[h, two_on] + other_got[h, two_on]
            one[h]["via_r"].start()
            one[h]["via_l"].start()
            half_wait(h, 1).wait_recv()
            part[h, one_on] = part[h, one_on] + other_got[h, one_on]
            one[h]["direct_r"].start()
            half_wait(h, 2).wait_recv()
            part[h, one_back] = part[h, one_back] + other_got[h, one_back]
            one[h]["direct_l"].start()

    def stat_copy(level, got, peer, slot, base, i):
        return remote(stat.at[level], got.at[slot], stat_s.at[base + i], stat_r.at[base + i], peer(i)[1])

    def stat_x(i, arriving=False):
        return stat_copy(1, stat_1, x_peer, lax.rem(x + NX - i, NX) if arriving else x, 0, i)

    def stat_y(i, arriving=False):
        return stat_copy(2, stat_2, y_peer, lax.rem(y + NY - i, NY) if arriving else y, 3, i)

    def stat_z(i, arriving=False):
        return stat_copy(3, stat_3, z_peer, lax.rem(z + NZ - i, NZ) if arriving else z, 6, i)

    def summed(got, n):
        return functools.reduce(lambda p, q: p + q, [got[i] for i in range(n)])

    stat_pair.wait_recv()
    stat[1] = stat[0] + stat_c[...]

    @pl.loop(1, NX)
    def _(i):
        stat_x(i).start()

    for h in range(H):
        with scope("n_via%d" % h):
            one[h]["via_r"].wait_recv()
            part[h, one_on, lo] = part[h, one_on, lo] + via_l[h]
            one[h]["comb_r"].start()
            one[h]["via_l"].wait_recv()
            part[h, one_back, hi] = part[h, one_back, hi] + via_r[h]
            one[h]["comb_l"].start()

    def two_copy(h, i):
        e, dev = b_peer(i)
        return remote(sum1.at[h, e], got2.at[h, i - 1], two_s.at[h, i - 1], two_r.at[h, i - 1], dev)

    def three_copy(h, i):
        e, dev = z_peer(i)
        return remote(sum2.at[h, e], got3.at[h, i - 1], three_s.at[h, i - 1], three_r.at[h, i - 1], dev)

    for h in range(H):
        with scope("o_one%d" % h):
            half_wait(h, 3).wait_recv()
            for name in ("direct_r", "direct_l", "comb_r", "comb_l"):
                one[h][name].wait_recv()
            sum1[h] = (part[h, a] + other_got[h, a]) + (got_l[h] + got_r[h])

            @pl.loop(1, NX)
            def _(i):
                two_copy(h, i).start()

    @pl.loop(1, NX)
    def _(i):
        stat_x(i, True).wait_recv()

    stat_1[x] = stat[1]
    stat[2] = summed(stat_1, NX)

    @pl.loop(1, NX)
    def _(i):
        stat_y(i).start()

    for h in range(H):
        with scope("p_two%d" % h):

            @pl.loop(1, NX)
            def _(i):
                two_copy(h, i).wait_recv()

            sum2[h] = (sum1[h, b] + got2[h, 0]) + (got2[h, 1] + got2[h, 2])

            @pl.loop(1, NZ)
            def _(i):
                three_copy(h, i).start()

    @pl.loop(1, NX)
    def _(i):
        stat_y(i, True).wait_recv()

    stat_2[y] = stat[2]
    stat[3] = summed(stat_2, NY)

    @pl.loop(1, NZ)
    def _(i):
        stat_z(i).start()

    for h in range(H):
        with scope("q_three%d" % h):

            @pl.loop(1, NZ)
            def _(i):
                three_copy(h, i).wait_recv()

            total = sum2[h, z]
            for i in range(NZ - 1):
                total = total + got3[h, i]
            grad[:, h * W : (h + 1) * W] = total * (-1.0 / PATHS)

    with scope("r_stat"):

        @pl.loop(1, NZ)
        def _(i):
            stat_z(i, True).wait_recv()

        stat_3[z] = stat[3]
        sums_out[...] = summed(stat_3, NZ)

    with scope("s_drain"):
        pay_copy.wait_send()
        fx_copy.wait_send()
        stat_pair.wait_send()
        for h in range(H):
            inc_copy[h].wait_send()
            for j in range(NX):
                half_copy(h, j).wait_send()
            for copy in one[h].values():
                copy.wait_send()

            @pl.loop(1, NZ)
            def _(i):
                bl_copy(h, i).wait_send()
                fl_copy(h, i).wait_send()
                three_copy(h, i).wait_send()

            @pl.loop(1, NX)
            def _(i):
                two_copy(h, i).wait_send()

        @pl.loop(1, NX)
        def _(i):
            stat_x(i).wait_send()
            stat_y(i).wait_send()

        @pl.loop(1, NZ)
        def _(i):
            stat_z(i).wait_send()


def finish(raw, sums, grad, bound, spread):
    mean = sums[0:1] * (1.0 / PATHS)
    grad[...] = raw[...]
    bound[...] = mean
    spread[...] = sums[1:2] * (1.0 / PATHS) - mean * mean


def shards(features, payoff, coefficients, exercise):
    dma = pltpu.SemaphoreType.DMA
    vmem = pltpu.VMEM
    arguments = [
        pltpu.with_memory_space_constraint(v, pltpu.HBM) for v in (features, payoff, coefficients, exercise)
    ]
    raw, sums = pl.pallas_call(
        body,
        name="dual_bound",
        out_shape=(jax.ShapeDtypeStruct((R, C), F32), jax.ShapeDtypeStruct((R, C), F32)),
        in_specs=[pl.BlockSpec(memory_space=pltpu.MemorySpace.HBM)] * 4,
        out_specs=[pl.BlockSpec(memory_space=pltpu.VMEM)] * 2,
        scratch_shapes=[
            vmem((2, 128, K), BF16),
            vmem((K, C), BF16),
            vmem((2, 128, C), F32),
            vmem((2, C), jnp.int32),
            vmem((2, 128, C), F32),
            vmem((2, 64, C), F32),
            vmem((H, 2, 128, W), F32),
            vmem((H, 2, 64, W), F32),
            vmem((2, 64, K), F32),
            vmem((2, 64, K), F32),
            vmem((4, 64, K), BF16),
            vmem((2, K // 2, 256), BF16),
            vmem((H, 4, 64, W), F32),
            vmem((H, NZ, 2, R, W), F32),
            vmem((H, NZ, 2, R, W), F32),
            vmem((H, NZ, 2, R, W), F32),
            vmem((H, NZ, 2, R, W), F32),
            vmem((H, NX, NY, NZ, R, W), F32),
            vmem((H, NX, NY, NZ, R, W), F32),
            vmem((H, NX, NY, NZ, R, W), F32),
            vmem((H, NY // 2, NZ, R, W), F32),
            vmem((H, NY // 2, NZ, R, W), F32),
            vmem((H, NY, NZ, R, W), F32),
            vmem((H, NY, NZ, R, W), F32),
            vmem((H, NY, NZ, R, W), F32),
            vmem((H, NY - 1, NZ, R, W), F32),
            vmem((H, NZ, R, W), F32),
            vmem((H, NZ - 1, R, W), F32),
            vmem((4, R, C), F32),
            vmem((R, C), F32),
            vmem((NX, R, C), F32),
            vmem((NY, R, C), F32),
            vmem((NZ, R, C), F32),
            dma((4,)),
            dma((4,)),
            dma((4,)),
            dma((H, NZ - 1)),
            dma((H, NZ - 1)),
            dma((H, NZ - 1)),
            dma((H, NZ - 1)),
            dma((H, NX)),
            dma((H, NX)),
            dma((H, 6)),
            dma((H, 6)),
            dma((H, NY - 1)),
            dma((H, NY - 1)),
            dma((H, NZ - 1)),
            dma((H, NZ - 1)),
            dma((14,)),
            dma((14,)),
        ],
        compiler_params=pltpu.CompilerParams(
            collective_id=0, has_side_effects=True, vmem_limit_bytes=40 * 1024 * 1024
        ),
    )(*arguments)
    grad, bound, spread = pl.pallas_call(
        finish,
        name="finish",
        out_shape=(
            jax.ShapeDtypeStruct((R, C), F32),
            jax.ShapeDtypeStruct((1, C), F32),
            jax.ShapeDtypeStruct((1, C), F32),
        ),
        compiler_params=pltpu.CompilerParams(vmem_limit_bytes=1024 * 1024),
    )(raw, sums)
    return grad, bound.reshape(C), spread.reshape(C)


def solution(mesh):
    torus = Mesh(mesh.devices.reshape(NZ, NC, NX, NY), AXES)
    in_specs = (P(DATE, PATH, None), P(DATE, PATH, None), P(), P(DATE, None))
    out_specs = (P(DATE + PATH, None), P(), P())
    return jax.shard_map(
        shards, mesh=torus, in_specs=in_specs, out_specs=out_specs, check_vma=False
    )
```

time: 256 us -> 43.5 us (0.17)
  the two profiles are of different devices: /device:TPU:1 before, /device:TPU:6 now
where the time goes in v2:
time: 43.5 us; the launch traced here: 43.4 us
  Pallas kernels  42.8 us (98%)
  between operations  0.64 us (1%)
    pallas_call x1, Pallas kernels, shards(): pl.pallas_call(body, name='dual_bound', out_shape=(jax.ShapeDtypeStruct((...  42.2 us

profile of v2, /device:TPU:6, one launch (start us, length us, event | category | flops | bytes accessed | tf_op | source)
XLA Modules:
  0.0 43.4 jit_solution(14375489029980915942)
XLA Ops:
  0.6 42.2 %dual_bound.1 = (f32[8,256]{1,0:T(8,128)S(1)}, f32[8,256]{1,0:T(8,128)S(1)}) custom-call(bf16[2,128,2048]{2,1,0:T(8,128)(2,1)} %feat.1, f32[2,128,256]{2,1,0:T(8,128)} %pay.1, bf16[2048,256]{1,0:T(8,128)(2,1)} %coef.1, s32[2,256]{1,0:T(2,128)} %exer.1), custom_call_target="tpu_custom_call" | custom-call | tf_op jit(solution)/shard_map/dual_bound/pallas_call | solution.py:494
  42.8 0.6 %finish.1 = (f32[8,256]{1,0:T(8,128)}, f32[1,256]{1,0:T(1,128)}, f32[1,256]{1,0:T(1,128)}) custom-call(f32[8,256]{1,0:T(8,128)S(1)} %get-tuple-element.8.raw, f32[8,256]{1,0:T(8,128)S(1)} %get-tuple-element.9.sums), custom_call_target="tpu_custom_call" | custom-call | tf_op jit(solution)/shard_map/finish/pallas_call | solution.py:556

commit v3 on v2

v3 whole, which is shorter than its diff:
```python
import functools

import jax
import jax.numpy as jnp
from jax import lax
from jax.experimental import pallas as pl
from jax.experimental.pallas import tpu as pltpu
from jax.sharding import Mesh
from jax.sharding import PartitionSpec as P

DATE = ("z", "core")
PATH = ("x", "y")
AXES = ("z", "core", "x", "y")
NZ, NC, NX, NY = 8, 2, 4, 4
TEMP = 0.25
MASKED = -1e30 * TEMP
PATHS = 2048
K = 2048
C = 256
R = 8
H = 2
W = C // H
F32 = jnp.float32
BF16 = jnp.bfloat16
MESH = pl.DeviceIdType.MESH
PIECES = 2
ORDER = (2, 1, 3, 0)
FAR_FIRST = (4, 3, 5, 2, 6, 1, 7)


def scope(name):
    return jax.named_scope(name)


def body(
    feat,
    pay,
    coef,
    exer,
    grad,
    sums_out,
    fbuf,
    cbuf,
    pbuf,
    ebuf,
    mpay,
    pay_got,
    inc,
    inc_got,
    fx_send,
    fx_got,
    fall,
    ft,
    rel,
    bl,
    bl_all,
    fl,
    fl_in,
    other_part,
    other_got,
    part,
    via_l,
    via_r,
    got_l,
    got_r,
    sum1,
    got2,
    sum2,
    got3,
    stat,
    stat_c,
    stat_1,
    stat_2,
    stat_3,
    load_sem,
    send,
    pair_s,
    pair_r,
    bl_r,
    fl_r,
    half_r,
    one_r,
    two_r,
    three_r,
    stat_r,
):
    z, core, x, y = (lax.axis_index(a) for a in AXES)
    other = 1 - core

    a = (1 - core) * x + core * y
    b = (1 - core) * y + core * x
    a_other = (1 - other) * x + other * y

    def along_a(e):
        return (z, core, (1 - core) * e + core * x, (1 - core) * y + core * e)

    def along_b(e):
        return (z, core, (1 - core) * x + core * e, (1 - core) * e + core * y)

    partner = (z, other, x, y)
    right, left = along_a(lax.rem(a + 1, NX)), along_a(lax.rem(a + NX - 1, NX))

    def b_peer(i):
        e = lax.rem(b + i, NX)
        return e, along_b(e)

    def z_peer(i):
        e = lax.rem(z + i, NZ)
        return e, (e, core, x, y)

    def x_peer(i):
        e = lax.rem(x + i, NX)
        return e, (z, core, e, y)

    def y_peer(i):
        e = lax.rem(y + i, NY)
        return e, (z, core, x, e)

    def remote(src, dst, ssem, rsem, device):
        return pltpu.make_async_remote_copy(src, dst, ssem, rsem, device_id=device, device_id_type=MESH)

    def greet(device):
        pl.semaphore_signal(barrier, inc=1, device_id=device, device_id_type=MESH)

    barrier = pltpu.get_barrier_semaphore()
    with scope("a_signal"):
        for i in FAR_FIRST:
            greet(z_peer(i)[1])
        for i in (2, 1, 3):
            greet(x_peer(i)[1])
            greet(y_peer(i)[1])
        greet(partner)

    depth = K // PIECES

    def piece(n):
        return slice(n * depth, (n + 1) * depth)

    loads = []
    for n in range(PIECES):
        loads.append(pltpu.make_async_copy(coef.at[piece(n), :], cbuf.at[piece(n), :], load_sem.at[2 * n]))
        loads.append(pltpu.make_async_copy(feat.at[:, :, piece(n)], fbuf.at[:, :, piece(n)], load_sem.at[2 * n + 1]))
    loads.append(pltpu.make_async_copy(exer, ebuf, load_sem.at[2 * PIECES]))
    loads.append(pltpu.make_async_copy(pay, pbuf, load_sem.at[2 * PIECES + 1]))
    for copy in loads:
        copy.start()

    with scope("b_mm1"):
        incs = None
        for n in range(PIECES):
            loads[2 * n].wait()
            loads[2 * n + 1].wait()
            flat = fbuf[:, :, piece(n)].reshape(2 * 128, depth)
            term = jnp.dot(flat, cbuf[piece(n), :], preferred_element_type=F32)
            incs = term if incs is None else incs + term
        for h in range(H):
            inc[h] = incs[:, h * W : (h + 1) * W].reshape(2, 128, W)

    with scope("c_mask"):
        loads[2 * PIECES].wait()
        loads[2 * PIECES + 1].wait()
        for t in range(2):
            mpay[t] = jnp.where(ebuf[t : t + 1] > 0, pbuf[t], MASKED)

    with scope("d_barrier"):
        pl.semaphore_wait(barrier, 1 + NZ - 1 + 2 * (NX - 1))

    own_half = pl.ds(pl.multiple_of(core * 64, 64), 64)
    other_half = pl.ds(pl.multiple_of(other * 64, 64), 64)

    pay_copy = remote(mpay.at[:, other_half, :], pay_got, pair_s.at[0], pair_r.at[0], partner)
    inc_copy = [
        remote(inc.at[h, :, other_half, :], inc_got.at[h], pair_s.at[1], pair_r.at[1 + h], partner) for h in range(H)
    ]
    pay_copy.start()
    for copy in inc_copy:
        copy.start()

    with scope("e_convert"):
        for t in range(2):
            fx_send[t] = fbuf[t, other_half, :].astype(F32)
            fall[2 * core + t] = fbuf[t, own_half, :]

    def bl_copy(h, i):
        e, dev = z_peer(i)
        return remote(bl.at[h, e], bl_all.at[h, i], send.at[0], bl_r.at[h], dev)

    def fl_copy(h, i):
        e, dev = z_peer(i)
        return remote(fl.at[h, e], fl_in.at[h, i], send.at[1], fl_r.at[h], dev)

    def arrived(ref, sem):
        pltpu.make_async_copy(ref, ref, sem).wait()

    def from_z(s):
        return lax.rem(z + NZ - s, NZ)

    pay_copy.wait_recv()
    for h in range(H):
        with scope("f_blocks%d" % h):
            cols = pl.ds(h * W, W)
            inc_copy[h].wait_recv()
            first = core == 0
            run = jnp.zeros((64, W), F32)
            us = []
            for t in range(4):
                mine_inc, got_inc = inc[h, t % 2, own_half, :], inc_got[h, t % 2]
                mine_pay, got_pay = mpay[t % 2, own_half, cols], pay_got[t % 2, :, cols]
                own = first if t < 2 else jnp.logical_not(first)
                run = run + jnp.where(own, mine_inc, got_inc)
                us.append((jnp.where(own, mine_pay, got_pay) - run) / TEMP)
            top = functools.reduce(jnp.maximum, us)
            lse = top + jnp.log(functools.reduce(lambda p, q: p + q, [jnp.exp(u - top) for u in us]))
            for t in range(4):
                rel[h, t] = us[t]
            for s in range(NZ):
                bl[h, s, 0] = run[s * R : (s + 1) * R]
                bl[h, s, 1] = lse[s * R : (s + 1) * R]

            for i in FAR_FIRST:
                bl_copy(h, i).start()

            bl_all[h, 0] = bl[h, z]

    fx_copy = remote(fx_send, fx_got, pair_s.at[2], pair_r.at[3], partner)
    fx_copy.start()
    with scope("g_features"):
        fx_copy.wait_recv()
        for t in range(2):
            fall[2 * other + t] = fx_got[t].astype(BF16)
        for k in range(8):
            strip = fall[:, :, k * 256 : (k + 1) * 256].reshape(256, 256).T
            for which in range(2):
                ft[which, k * 128 : (k + 1) * 128, :] = strip[which * 128 : (which + 1) * 128]

    stat[0] = jnp.zeros((R, C), F32)
    for h in range(H):
        with scope("h_blwait%d" % h):

            arrived(bl_all.at[h, pl.ds(1, NZ - 1)], bl_r.at[h])

        with scope("i_owner%d" % h):
            cols = slice(h * W, (h + 1) * W)
            before = jnp.zeros((R, W), F32)
            befores, ss = [], []
            for s in range(NZ):
                shift = before / TEMP
                befores.append(shift)
                ss.append(bl_all[h, from_z(s), 1] - shift)
                before = before + bl_all[h, from_z(s), 0]
            peak = functools.reduce(jnp.maximum, ss)
            lse = peak + jnp.log(functools.reduce(lambda p, q: p + q, [jnp.exp(s - peak) for s in ss]))
            later = jnp.zeros((R, W), F32)
            for s in reversed(range(NZ)):
                fl[h, s, 0] = lse + befores[s]
                fl[h, s, 1] = later
                later = later + jnp.exp(ss[s] - lse)
            smoothed = TEMP * lse
            stat[0, 0:1, cols] = jnp.sum(smoothed, axis=0, keepdims=True)
            stat[0, 1:2, cols] = jnp.sum(smoothed * smoothed, axis=0, keepdims=True)

            for i in FAR_FIRST:
                fl_copy(h, i).start()

            fl_in[h, 0] = fl[h, z]

    def stat_x(i):
        return remote(stat.at[0], stat_1.at[i], send.at[2], stat_r.at[0], x_peer(i)[1])

    def stat_y(i):
        return remote(stat.at[1], stat_2.at[i], send.at[2], stat_r.at[1], y_peer(i)[1])

    def stat_z(i):
        return remote(stat.at[2], stat_3.at[i], send.at[3], stat_r.at[2], z_peer(i)[1])

    def summed(got, here, n):
        return functools.reduce(lambda p, q: p + q, [got[lax.rem(here + n - s, n)] for s in range(n)])

    stat_1[0] = stat[0]
    for i in (2, 1, 3):
        stat_x(i).start()

    stat_pair = remote(stat.at[3], stat_c, send.at[2], stat_r.at[3], partner)

    def half_copy(h, j):
        chunk = lax.rem(a_other + ORDER[j], NX)
        return remote(other_part.at[h, chunk], other_got.at[h, j], send.at[4], half_r.at[h, min(j, 1)], partner)

    lo, hi = pl.ds(0, NY // 2), pl.ds(NY // 2, NY // 2)
    two_on = lax.rem(a + 2, NX)
    one_on = lax.rem(a + 1, NX)
    one_back = lax.rem(a + 3, NX)

    def one_copies(h):
        return dict(
            via_r=remote(part.at[h, two_on, lo], via_l.at[h], send.at[5], one_r.at[h, 0], right),
            via_l=remote(part.at[h, two_on, hi], via_r.at[h], send.at[5], one_r.at[h, 1], left),
            direct_r=remote(part.at[h, one_on, hi], got_l.at[h, hi], send.at[5], one_r.at[h, 2], right),
            direct_l=remote(part.at[h, one_back, lo], got_r.at[h, lo], send.at[5], one_r.at[h, 3], left),
            comb_r=remote(part.at[h, one_on, lo], got_l.at[h, lo], send.at[5], one_r.at[h, 2], right),
            comb_l=remote(part.at[h, one_back, hi], got_r.at[h, hi], send.at[5], one_r.at[h, 3], left),
        )

    one = [one_copies(h) for h in range(H)]

    def product(h, which, tail, out):
        for n in range(2):
            block = jnp.dot(ft[which, n * 512 : (n + 1) * 512, :], tail, preferred_element_type=F32)
            for k in range(4):
                for p in range(NX):
                    for q in range(NY):
                        row = k * 128 + (p * NY + q) * R
                        out[h, (1 - which) * p + which * q, (1 - which) * q + which * p, n * 4 + k] = block[row : row + R]

    for h in range(H):
        with scope("j_flwait%d" % h):

            arrived(fl_in.at[h, pl.ds(1, NZ - 1)], fl_r.at[h])

        with scope("k_mm2a%d" % h):
            level = jnp.concatenate([fl_in[h, from_z(s), 0] for s in range(NZ)], axis=0)
            run = jnp.concatenate([fl_in[h, from_z(s), 1] for s in range(NZ)], axis=0)
            tails = [None] * 4
            for t in reversed(range(4)):
                run = run + jnp.exp(rel[h, t] - level)
                tails[t] = run.astype(BF16)
            tail = jnp.concatenate(tails, axis=0)
            product(h, other, tail, other_part)
            for j in range(NX):
                half_copy(h, j).start()
        with scope("l_mm2b%d" % h):
            product(h, core, tail, part)
        if h == 0:
            arrived(stat_1.at[pl.ds(1, NX - 1)], stat_r.at[0])
            stat[1] = summed(stat_1, x, NX)
            stat_2[0] = stat[1]
            for i in (2, 1, 3):
                stat_y(i).start()

    def joined(h, j):
        chunk = lax.rem(a + ORDER[j], NX)
        part[h, chunk] = part[h, chunk] + other_got[h, j]

    def begin(h):
        with scope("m_half%d" % h):
            arrived(other_got.at[h, 0], half_r.at[h, 0])
            joined(h, 0)
            one[h]["via_r"].start()
            one[h]["via_l"].start()

    def direct(h):
        with scope("n_direct%d" % h):
            arrived(other_got.at[h, pl.ds(1, NX - 1)], half_r.at[h, 1])
            joined(h, 1)
            one[h]["direct_r"].start()
            joined(h, 2)
            one[h]["direct_l"].start()

    def combine(h):
        with scope("n_via%d" % h):
            one[h]["via_r"].wait_recv()
            part[h, one_on, lo] = part[h, one_on, lo] + via_l[h]
            one[h]["comb_r"].start()
            one[h]["via_l"].wait_recv()
            part[h, one_back, hi] = part[h, one_back, hi] + via_r[h]
            one[h]["comb_l"].start()

    begin(0)
    direct(0)
    begin(1)
    combine(0)
    direct(1)
    with scope("o_stat"):
        arrived(stat_2.at[pl.ds(1, NY - 1)], stat_r.at[1])
        stat[2] = summed(stat_2, y, NY)
        stat_3[0] = stat[2]
        for i in FAR_FIRST:
            stat_z(i).start()
    combine(1)

    def two_copy(h, i):
        e, dev = b_peer(i)
        return remote(sum1.at[h, e], got2.at[h, i - 1], send.at[6], two_r.at[h], dev)

    def three_copy(h, i):
        e, dev = z_peer(i)
        return remote(sum2.at[h, e], got3.at[h, i - 1], send.at[7], three_r.at[h], dev)

    for h in range(H):
        with scope("o_one%d" % h):
            arrived(got_l.at[h], one_r.at[h, 2])
            arrived(got_r.at[h], one_r.at[h, 3])
            sum1[h] = (part[h, a] + other_got[h, 3]) + (got_l[h] + got_r[h])
            for i in (2, 1, 3):
                two_copy(h, i).start()

    for h in range(H):
        with scope("p_two%d" % h):
            arrived(got2.at[h], two_r.at[h])
            sum2[h] = (sum1[h, b] + got2[h, 0]) + (got2[h, 1] + got2[h, 2])

            for i in FAR_FIRST:
                three_copy(h, i).start()

    with scope("q_stat"):
        arrived(stat_3.at[pl.ds(1, NZ - 1)], stat_r.at[2])
        stat[3] = summed(stat_3, z, NZ)
        stat_pair.start()

    for h in range(H):
        with scope("q_three%d" % h):
            arrived(got3.at[h], three_r.at[h])
            total = sum2[h, z]
            for i in range(NZ - 1):
                total = total + got3[h, i]
            grad[:, h * W : (h + 1) * W] = total * (-1.0 / PATHS)

    with scope("r_stat"):
        arrived(stat_c, stat_r.at[3])
        sums_out[...] = stat[3] + stat_c[...]

    with scope("s_drain"):
        pay_copy.wait_send()
        arrived(inc_got, pair_s.at[1])
        fx_copy.wait_send()
        arrived(bl.at[:, pl.ds(0, NZ - 1)], send.at[0])
        arrived(fl.at[:, pl.ds(0, NZ - 1)], send.at[1])
        arrived(stat_3.at[pl.ds(0, 7)], send.at[2])
        arrived(stat_3.at[pl.ds(0, 7)], send.at[3])
        arrived(other_part, send.at[4])
        arrived(part.at[:, pl.ds(0, NX - 1)], send.at[5])
        arrived(sum1.at[:, pl.ds(0, NY - 1)], send.at[6])
        arrived(sum2.at[:, pl.ds(0, NZ - 1)], send.at[7])


def finish(raw, sums, grad, bound, spread):
    mean = sums[0:1] * (1.0 / PATHS)
    grad[...] = raw[...]
    bound[...] = mean
    spread[...] = sums[1:2] * (1.0 / PATHS) - mean * mean


def shards(features, payoff, coefficients, exercise):
    dma = pltpu.SemaphoreType.DMA
    vmem = pltpu.VMEM
    arguments = [
        pltpu.with_memory_space_constraint(v, pltpu.HBM) for v in (features, payoff, coefficients, exercise)
    ]
    raw, sums = pl.pallas_call(
        body,
        name="dual_bound",
        out_shape=(jax.ShapeDtypeStruct((R, C), F32), jax.ShapeDtypeStruct((R, C), F32)),
        in_specs=[pl.BlockSpec(memory_space=pltpu.MemorySpace.HBM)] * 4,
        out_specs=[pl.BlockSpec(memory_space=pltpu.VMEM)] * 2,
        scratch_shapes=[
            vmem((2, 128, K), BF16),
            vmem((K, C), BF16),
            vmem((2, 128, C), F32),
            vmem((2, C), jnp.int32),
            vmem((2, 128, C), F32),
            vmem((2, 64, C), F32),
            vmem((H, 2, 128, W), F32),
            vmem((H, 2, 64, W), F32),
            vmem((2, 64, K), F32),
            vmem((2, 64, K), F32),
            vmem((4, 64, K), BF16),
            vmem((2, K // 2, 256), BF16),
            vmem((H, 4, 64, W), F32),
            vmem((H, NZ, 2, R, W), F32),
            vmem((H, NZ, 2, R, W), F32),
            vmem((H, NZ, 2, R, W), F32),
            vmem((H, NZ, 2, R, W), F32),
            vmem((H, NX, NY, NZ, R, W), F32),
            vmem((H, NX, NY, NZ, R, W), F32),
            vmem((H, NX, NY, NZ, R, W), F32),
            vmem((H, NY // 2, NZ, R, W), F32),
            vmem((H, NY // 2, NZ, R, W), F32),
            vmem((H, NY, NZ, R, W), F32),
            vmem((H, NY, NZ, R, W), F32),
            vmem((H, NY, NZ, R, W), F32),
            vmem((H, NY - 1, NZ, R, W), F32),
            vmem((H, NZ, R, W), F32),
            vmem((H, NZ - 1, R, W), F32),
            vmem((4, R, C), F32),
            vmem((R, C), F32),
            vmem((NX, R, C), F32),
            vmem((NY, R, C), F32),
            vmem((NZ, R, C), F32),
            dma((2 * PIECES + 2,)),
            dma((8,)),
            dma((3,)),
            dma((4,)),
            dma((H,)),
            dma((H,)),
            dma((H, 2)),
            dma((H, 4)),
            dma((H,)),
            dma((H,)),
            dma((4,)),
        ],
        compiler_params=pltpu.CompilerParams(
            collective_id=0, has_side_effects=True, vmem_limit_bytes=40 * 1024 * 1024
        ),
    )(*arguments)
    grad, bound, spread = pl.pallas_call(
        finish,
        name="finish",
        out_shape=(
            jax.ShapeDtypeStruct((R, C), F32),
            jax.ShapeDtypeStruct((1, C), F32),
            jax.ShapeDtypeStruct((1, C), F32),
        ),
        compiler_params=pltpu.CompilerParams(vmem_limit_bytes=1024 * 1024),
    )(raw, sums)
    return grad, bound.reshape(C), spread.reshape(C)


def solution(mesh):
    torus = Mesh(mesh.devices.reshape(NZ, NC, NX, NY), AXES)
    in_specs = (P(DATE, PATH, None), P(DATE, PATH, None), P(), P(DATE, None))
    out_specs = (P(DATE + PATH, None), P(), P())
    return jax.shard_map(
        shards, mesh=torus, in_specs=in_specs, out_specs=out_specs, check_vma=False
    )
```

time: 43.5 us -> 41.3 us (0.949)
  Pallas kernels: 42.8 us -> 40.6 us
    pallas_call x1, Pallas kernels: 42.2 us -> 40 us  [shards(): pl.pallas_call(body, name='dual_bound', out_shape=(jax.ShapeDtypeStruct((...]
where the time goes in v3:
time: 41.3 us; the launch traced here: 41.2 us
  Pallas kernels  40.6 us (98%)
  between operations  0.64 us (2%)
    pallas_call x1, Pallas kernels, shards(): pl.pallas_call(body, name='dual_bound', out_shape=(jax.ShapeDtypeStruct((...  40 us

profile of v3, /device:TPU:6, one launch (start us, length us, event | category | flops | bytes accessed | tf_op | source)
XLA Modules:
  0.0 41.2 jit_solution(7415176639088681739)
XLA Ops:
  0.6 40.0 %dual_bound.1 = (f32[8,256]{1,0:T(8,128)S(1)}, f32[8,256]{1,0:T(8,128)S(1)}) custom-call(bf16[2,128,2048]{2,1,0:T(8,128)(2,1)} %feat.1, f32[2,128,256]{2,1,0:T(8,128)} %pay.1, bf16[2048,256]{1,0:T(8,128)(2,1)} %coef.1, s32[2,256]{1,0:T(2,128)} %exer.1), custom_call_target="tpu_custom_call" | custom-call | tf_op jit(solution)/shard_map/dual_bound/pallas_call | solution.py:449
  40.6 0.6 %finish.1 = (f32[8,256]{1,0:T(8,128)}, f32[1,256]{1,0:T(1,128)}, f32[1,256]{1,0:T(1,128)}) custom-call(f32[8,256]{1,0:T(8,128)S(1)} %get-tuple-element.8.raw, f32[8,256]{1,0:T(8,128)S(1)} %get-tuple-element.9.sums), custom_call_target="tpu_custom_call" | custom-call | tf_op jit(solution)/shard_map/finish/pallas_call | solution.py:505

commit v4 on v3

--- a/solution.py
+++ b/solution.py
@@ -24,7 +24,6 @@
 BF16 = jnp.bfloat16
 MESH = pl.DeviceIdType.MESH
 PIECES = 2
-ORDER = (2, 1, 3, 0)
 FAR_FIRST = (4, 3, 5, 2, 6, 1, 7)
 
 
@@ -43,21 +42,19 @@
     cbuf,
     pbuf,
     ebuf,
-    mpay,
-    pay_got,
-    inc,
-    inc_got,
+    both,
+    both_got,
     fx_send,
-    fx_got,
     fall,
+    ft32,
     ft,
     rel,
     bl,
     bl_all,
     fl,
     fl_in,
-    other_part,
-    other_got,
+    tails,
+    tail_got,
     part,
     via_l,
     via_r,
@@ -154,13 +151,15 @@
             term = jnp.dot(flat, cbuf[piece(n), :], preferred_element_type=F32)
             incs = term if incs is None else incs + term
         for h in range(H):
-            inc[h] = incs[:, h * W : (h + 1) * W].reshape(2, 128, W)
+            both[h, 1] = incs[:, h * W : (h + 1) * W].reshape(2, 128, W)
 
     with scope("c_mask"):
         loads[2 * PIECES].wait()
         loads[2 * PIECES + 1].wait()
         for t in range(2):
-            mpay[t] = jnp.where(ebuf[t : t + 1] > 0, pbuf[t], MASKED)
+            masked = jnp.where(ebuf[t : t + 1] > 0, pbuf[t], MASKED)
+            for h in range(H):
+                both[h, 0, t] = masked[:, h * W : (h + 1) * W]
 
     with scope("d_barrier"):
         pl.semaphore_wait(barrier, 1 + NZ - 1 + 2 * (NX - 1))
@@ -168,18 +167,11 @@
     own_half = pl.ds(pl.multiple_of(core * 64, 64), 64)
     other_half = pl.ds(pl.multiple_of(other * 64, 64), 64)
 
-    pay_copy = remote(mpay.at[:, other_half, :], pay_got, pair_s.at[0], pair_r.at[0], partner)
-    inc_copy = [
-        remote(inc.at[h, :, other_half, :], inc_got.at[h], pair_s.at[1], pair_r.at[1 + h], partner) for h in range(H)
+    both_copy = [
+        remote(both.at[h, :, :, other_half, :], both_got.at[h], pair_s.at[0], pair_r.at[h], partner) for h in range(H)
     ]
-    pay_copy.start()
-    for copy in inc_copy:
+    for copy in both_copy:
         copy.start()
-
-    with scope("e_convert"):
-        for t in range(2):
-            fx_send[t] = fbuf[t, other_half, :].astype(F32)
-            fall[2 * core + t] = fbuf[t, own_half, :]
 
     def bl_copy(h, i):
         e, dev = z_peer(i)
@@ -195,17 +187,15 @@
     def from_z(s):
         return lax.rem(z + NZ - s, NZ)
 
-    pay_copy.wait_recv()
     for h in range(H):
         with scope("f_blocks%d" % h):
-            cols = pl.ds(h * W, W)
-            inc_copy[h].wait_recv()
+            arrived(both_got.at[h], pair_r.at[h])
             first = core == 0
             run = jnp.zeros((64, W), F32)
             us = []
             for t in range(4):
-                mine_inc, got_inc = inc[h, t % 2, own_half, :], inc_got[h, t % 2]
-                mine_pay, got_pay = mpay[t % 2, own_half, cols], pay_got[t % 2, :, cols]
+                mine_pay, got_pay = both[h, 0, t % 2, own_half, :], both_got[h, 0, t % 2]
+                mine_inc, got_inc = both[h, 1, t % 2, own_half, :], both_got[h, 1, t % 2]
                 own = first if t < 2 else jnp.logical_not(first)
                 run = run + jnp.where(own, mine_inc, got_inc)
                 us.append((jnp.where(own, mine_pay, got_pay) - run) / TEMP)
@@ -222,16 +212,31 @@
 
             bl_all[h, 0] = bl[h, z]
 
-    fx_copy = remote(fx_send, fx_got, pair_s.at[2], pair_r.at[3], partner)
-    fx_copy.start()
+    fx_copy = remote(fx_send, fall.at[pl.ds(2 * core, 2)], pair_s.at[1], pair_r.at[2], partner)
+
+    with scope("g_convert"):
+        for n in range(NZ):
+            theirs = pl.ds(pl.multiple_of(n * 256 + other * 128, 128), 128)
+            for t in range(2):
+                fx_send[t, :, n * 128 : (n + 1) * 128] = fbuf[t, :, theirs].astype(F32)
+        fx_copy.start()
+        for n in range(NZ):
+            ours = pl.ds(pl.multiple_of(n * 256 + core * 128, 128), 128)
+            for t in range(2):
+                fall[2 * core + t, :, n * 128 : (n + 1) * 128] = fbuf[t, :, ours].astype(F32)
+
     with scope("g_features"):
-        fx_copy.wait_recv()
-        for t in range(2):
-            fall[2 * other + t] = fx_got[t].astype(BF16)
-        for k in range(8):
-            strip = fall[:, :, k * 256 : (k + 1) * 256].reshape(256, 256).T
-            for which in range(2):
-                ft[which, k * 128 : (k + 1) * 128, :] = strip[which * 128 : (which + 1) * 128]
+        arrived(fx_send, pair_r.at[2])
+        for side, rows in enumerate((own_half, other_half)):
+            for n in range(NZ):
+                strip = fall[:, rows, n * 128 : (n + 1) * 128].reshape(256, 128).T
+                for p in range(NX):
+                    for q in range(NY):
+                        row = (p * NY + q) * R
+                        to_a, to_b = (1 - core) * p + core * q, (1 - core) * q + core * p
+                        ft32[to_a, to_b, n] = strip[row : row + R]
+            for p in range(NX):
+                ft[side, p] = ft32[p].reshape(NY * NZ * R, 256).astype(BF16)
 
     stat[0] = jnp.zeros((R, C), F32)
     for h in range(H):
@@ -282,9 +287,7 @@
 
     stat_pair = remote(stat.at[3], stat_c, send.at[2], stat_r.at[3], partner)
 
-    def half_copy(h, j):
-        chunk = lax.rem(a_other + ORDER[j], NX)
-        return remote(other_part.at[h, chunk], other_got.at[h, j], send.at[4], half_r.at[h, min(j, 1)], partner)
+    tail_copy = [remote(tails.at[h], tail_got.at[h], send.at[4], half_r.at[h], partner) for h in range(H)]
 
     lo, hi = pl.ds(0, NY // 2), pl.ds(NY // 2, NY // 2)
     two_on = lax.rem(a + 2, NX)
@@ -292,81 +295,74 @@
     one_back = lax.rem(a + 3, NX)
 
     def one_copies(h):
-        return dict(
-            via_r=remote(part.at[h, two_on, lo], via_l.at[h], send.at[5], one_r.at[h, 0], right),
-            via_l=remote(part.at[h, two_on, hi], via_r.at[h], send.at[5], one_r.at[h, 1], left),
-            direct_r=remote(part.at[h, one_on, hi], got_l.at[h, hi], send.at[5], one_r.at[h, 2], right),
-            direct_l=remote(part.at[h, one_back, lo], got_r.at[h, lo], send.at[5], one_r.at[h, 3], left),
-            comb_r=remote(part.at[h, one_on, lo], got_l.at[h, lo], send.at[5], one_r.at[h, 2], right),
-            comb_l=remote(part.at[h, one_back, hi], got_r.at[h, hi], send.at[5], one_r.at[h, 3], left),
+        copies = dict(
+            direct_r=remote(part.at[h, one_on, hi], got_l.at[h, hi], send.at[5], one_r.at[h, 4], right),
+            direct_l=remote(part.at[h, one_back, lo], got_r.at[h, lo], send.at[5], one_r.at[h, 5], left),
         )
+        for n in range(NY // 2):
+            m = NY // 2 + n
+            copies["via_r%d" % n] = remote(part.at[h, two_on, n], via_l.at[h, n], send.at[5], one_r.at[h, n], right)
+            copies["via_l%d" % n] = remote(part.at[h, two_on, m], via_r.at[h, n], send.at[5], one_r.at[h, 2 + n], left)
+            copies["comb_r%d" % n] = remote(part.at[h, one_on, n], got_l.at[h, n], send.at[5], one_r.at[h, 4], right)
+            copies["comb_l%d" % n] = remote(part.at[h, one_back, m], got_r.at[h, m], send.at[5], one_r.at[h, 5], left)
+        return copies
 
     one = [one_copies(h) for h in range(H)]
 
-    def product(h, which, tail, out):
-        for n in range(2):
-            block = jnp.dot(ft[which, n * 512 : (n + 1) * 512, :], tail, preferred_element_type=F32)
-            for k in range(4):
-                for p in range(NX):
-                    for q in range(NY):
-                        row = k * 128 + (p * NY + q) * R
-                        out[h, (1 - which) * p + which * q, (1 - which) * q + which * p, n * 4 + k] = block[row : row + R]
-
-    for h in range(H):
+    def reverse_scan(h):
         with scope("j_flwait%d" % h):
-
             arrived(fl_in.at[h, pl.ds(1, NZ - 1)], fl_r.at[h])
-
-        with scope("k_mm2a%d" % h):
+        with scope("k_tails%d" % h):
             level = jnp.concatenate([fl_in[h, from_z(s), 0] for s in range(NZ)], axis=0)
             run = jnp.concatenate([fl_in[h, from_z(s), 1] for s in range(NZ)], axis=0)
-            tails = [None] * 4
             for t in reversed(range(4)):
                 run = run + jnp.exp(rel[h, t] - level)
-                tails[t] = run.astype(BF16)
-            tail = jnp.concatenate(tails, axis=0)
-            product(h, other, tail, other_part)
-            for j in range(NX):
-                half_copy(h, j).start()
-        with scope("l_mm2b%d" % h):
-            product(h, core, tail, part)
-        if h == 0:
-            arrived(stat_1.at[pl.ds(1, NX - 1)], stat_r.at[0])
-            stat[1] = summed(stat_1, x, NX)
-            stat_2[0] = stat[1]
-            for i in (2, 1, 3):
-                stat_y(i).start()
-
-    def joined(h, j):
-        chunk = lax.rem(a + ORDER[j], NX)
-        part[h, chunk] = part[h, chunk] + other_got[h, j]
+                tails[h, t] = run
+            tail_copy[h].start()
+
+    def own_paths(h):
+        with scope("k_mm2a%d" % h):
+            mine = tails[h].reshape(256, W).astype(BF16)
+            for p in range(NX):
+                part[h, p] = jnp.dot(ft[0, p], mine, preferred_element_type=F32).reshape(NY, NZ, R, W)
 
     def begin(h):
         with scope("m_half%d" % h):
-            arrived(other_got.at[h, 0], half_r.at[h, 0])
-            joined(h, 0)
-            one[h]["via_r"].start()
-            one[h]["via_l"].start()
+            arrived(tail_got.at[h], half_r.at[h])
+            theirs = tail_got[h].reshape(256, W).astype(BF16)
+            for p in range(NX):
+                term = jnp.dot(ft[1, p], theirs, preferred_element_type=F32)
+                part[h, p] = part[h, p] + term.reshape(NY, NZ, R, W)
+            for n in range(NY // 2):
+                one[h]["via_r%d" % n].start()
+                one[h]["via_l%d" % n].start()
 
     def direct(h):
-        with scope("n_direct%d" % h):
-            arrived(other_got.at[h, pl.ds(1, NX - 1)], half_r.at[h, 1])
-            joined(h, 1)
-            one[h]["direct_r"].start()
-            joined(h, 2)
-            one[h]["direct_l"].start()
+        one[h]["direct_r"].start()
+        one[h]["direct_l"].start()
 
     def combine(h):
         with scope("n_via%d" % h):
-            one[h]["via_r"].wait_recv()
-            part[h, one_on, lo] = part[h, one_on, lo] + via_l[h]
-            one[h]["comb_r"].start()
-            one[h]["via_l"].wait_recv()
-            part[h, one_back, hi] = part[h, one_back, hi] + via_r[h]
-            one[h]["comb_l"].start()
-
+            for n in range(NY // 2):
+                m = NY // 2 + n
+                one[h]["via_r%d" % n].wait_recv()
+                part[h, one_on, n] = part[h, one_on, n] + via_l[h, n]
+                one[h]["comb_r%d" % n].start()
+                one[h]["via_l%d" % n].wait_recv()
+                part[h, one_back, m] = part[h, one_back, m] + via_r[h, n]
+                one[h]["comb_l%d" % n].start()
+
+    reverse_scan(0)
+    own_paths(0)
+    arrived(stat_1.at[pl.ds(1, NX - 1)], stat_r.at[0])
+    stat[1] = summed(stat_1, x, NX)
+    stat_2[0] = stat[1]
+    for i in (2, 1, 3):
+        stat_y(i).start()
     begin(0)
     direct(0)
+    reverse_scan(1)
+    own_paths(1)
     begin(1)
     combine(0)
     direct(1)
@@ -388,9 +384,9 @@
 
     for h in range(H):
         with scope("o_one%d" % h):
-            arrived(got_l.at[h], one_r.at[h, 2])
-            arrived(got_r.at[h], one_r.at[h, 3])
-            sum1[h] = (part[h, a] + other_got[h, 3]) + (got_l[h] + got_r[h])
+            arrived(got_l.at[h], one_r.at[h, 4])
+            arrived(got_r.at[h], one_r.at[h, 5])
+            sum1[h] = part[h, a] + (got_l[h] + got_r[h])
             for i in (2, 1, 3):
                 two_copy(h, i).start()
 
@@ -420,14 +416,13 @@
         sums_out[...] = stat[3] + stat_c[...]
 
     with scope("s_drain"):
-        pay_copy.wait_send()
-        arrived(inc_got, pair_s.at[1])
+        arrived(both_got, pair_s.at[0])
         fx_copy.wait_send()
         arrived(bl.at[:, pl.ds(0, NZ - 1)], send.at[0])
         arrived(fl.at[:, pl.ds(0, NZ - 1)], send.at[1])
         arrived(stat_3.at[pl.ds(0, 7)], send.at[2])
         arrived(stat_3.at[pl.ds(0, 7)], send.at[3])
-        arrived(other_part, send.at[4])
+        arrived(tails, send.at[4])
         arrived(part.at[:, pl.ds(0, NX - 1)], send.at[5])
         arrived(sum1.at[:, pl.ds(0, NY - 1)], send.at[6])
         arrived(sum2.at[:, pl.ds(0, NZ - 1)], send.at[7])
@@ -457,21 +452,19 @@
             vmem((K, C), BF16),
             vmem((2, 128, C), F32),
             vmem((2, C), jnp.int32),
-            vmem((2, 128, C), F32),
-            vmem((2, 64, C), F32),
-            vmem((H, 2, 128, W), F32),
-            vmem((H, 2, 64, W), F32),
-            vmem((2, 64, K), F32),
-            vmem((2, 64, K), F32),
-            vmem((4, 64, K), BF16),
-            vmem((2, K // 2, 256), BF16),
+            vmem((H, 2, 2, 128, W), F32),
+            vmem((H, 2, 2, 64, W), F32),
+            vmem((2, 128, K // 2), F32),
+            vmem((4, 128, K // 2), F32),
+            vmem((NX, NY, NZ, R, 256), F32),
+            vmem((2, NX, NY * NZ * R, 256), BF16),
             vmem((H, 4, 64, W), F32),
             vmem((H, NZ, 2, R, W), F32),
             vmem((H, NZ, 2, R, W), F32),
             vmem((H, NZ, 2, R, W), F32),
             vmem((H, NZ, 2, R, W), F32),
-            vmem((H, NX, NY, NZ, R, W), F32),
-            vmem((H, NX, NY, NZ, R, W), F32),
+            vmem((H, 4, 64, W), F32),
+            vmem((H, 4, 64, W), F32),
             vmem((H, NX, NY, NZ, R, W), F32),
             vmem((H, NY // 2, NZ, R, W), F32),
             vmem((H, NY // 2, NZ, R, W), F32),
@@ -488,12 +481,12 @@
             vmem((NZ, R, C), F32),
             dma((2 * PIECES + 2,)),
             dma((8,)),
+            dma((2,)),
             dma((3,)),
-            dma((4,)),
             dma((H,)),
             dma((H,)),
-            dma((H, 2)),
-            dma((H, 4)),
+            dma((H,)),
+            dma((H, 6)),
             dma((H,)),
             dma((H,)),
             dma((4,)),

time: 41.3 us -> 39.6 us (0.959)
  Pallas kernels: 40.6 us -> 38.9 us
    pallas_call x1, Pallas kernels: 40 us -> 38.2 us  [shards(): pl.pallas_call(body, name='dual_bound', out_shape=(jax.ShapeDtypeStruct((...]
where the time goes in v4:
time: 39.6 us; the launch traced here: 39.5 us
  Pallas kernels  38.9 us (98%)
  between operations  0.64 us (2%)
    pallas_call x1, Pallas kernels, shards(): pl.pallas_call(body, name='dual_bound', out_shape=(jax.ShapeDtypeStruct((...  38.2 us

profile of v4, /device:TPU:6, one launch (start us, length us, event | category | flops | bytes accessed | tf_op | source)
XLA Modules:
  0.0 39.5 jit_solution(1083778751902733895)
XLA Ops:
  0.6 38.2 %dual_bound.1 = (f32[8,256]{1,0:T(8,128)S(1)}, f32[8,256]{1,0:T(8,128)S(1)}) custom-call(bf16[2,128,2048]{2,1,0:T(8,128)(2,1)} %feat.1, f32[2,128,256]{2,1,0:T(8,128)} %pay.1, bf16[2048,256]{1,0:T(8,128)(2,1)} %coef.1, s32[2,256]{1,0:T(2,128)} %exer.1), custom_call_target="tpu_custom_call" | custom-call | tf_op jit(solution)/shard_map/dual_bound/pallas_call | solution.py:444
  38.9 0.6 %finish.1 = (f32[8,256]{1,0:T(8,128)}, f32[1,256]{1,0:T(1,128)}, f32[1,256]{1,0:T(1,128)}) custom-call(f32[8,256]{1,0:T(8,128)S(1)} %get-tuple-element.8.raw, f32[8,256]{1,0:T(8,128)S(1)} %get-tuple-element.9.sums), custom_call_target="tpu_custom_call" | custom-call | tf_op jit(solution)/shard_map/finish/pallas_call | solution.py:498
